TPU v7x, 32 devices: a whole 2x2x4 slice. The times are simulated.
32 devices in a mesh: group: 2 (over x), engine: 4 (over y, core), chan: 4 (over z).
Axes of the slice: x: 2, y: 2, z: 4, core: 2. Of those that a mesh axis runs over, the one named last changes fastest.
Arguments:
- mr_qkv: bfloat16 [2, 3, 128, 8192], P(None, None, ('group', 'engine'), 'chan'), parts along dimension 2, may hold values from -6 to 6
- li_qkv: bfloat16 [2, 3, 128, 8192], P(None, None, ('group', 'engine'), 'chan'), parts along dimension 2, may hold values from -6 to 6
- conv_tails: bfloat16 [128, 127, 8192], P(('group', 'engine'), None, 'chan'), parts along dimension 0, may hold values from -6 to 6
- modal_states: float32 [128, 16, 8192], P(('group', 'engine'), None, 'chan'), parts along dimension 0, may hold values from -12 to 12
- source: int32 [128], P('group'), parts along dimension 0, may hold values from 0 to 63, as said below
- remaining: int32 [128], P(('group', 'engine')), parts along dimension 0, may hold values from 0 to 3
- mr_filter: bfloat16 [128, 8192], P(None, 'chan'), may hold values from -0.5 to 0.5
- li_decay: float32 [16, 8192], P(None, 'chan'), may hold values from 0.5 to 0.999
- li_residue: float32 [16, 8192], P(None, 'chan'), may hold values from -1.5 to 1.5
- mr_panels: bfloat16 [8, 8192, 512], P('engine', 'chan'), may hold values from -0.046875 to 0.046875
- li_panels: bfloat16 [8, 8192, 512], P('engine', 'chan'), may hold values from -0.046875 to 0.046875
- panel_slot: int32 [8], replicated, may hold values from 0 to 7, each once
Outputs:
- mixed: bfloat16 [2, 128, 4096], P(None, ('group', 'engine'), 'chan'), parts along dimension 1
- new_tails: bfloat16 [128, 127, 8192], P(('group', 'engine'), None, 'chan'), parts along dimension 0
- new_states: float32 [128, 16, 8192], P(('group', 'engine'), None, 'chan'), parts along dimension 0
There are 2 independent parts, one for each index of `group`. A program takes and returns all parts, laid end to end along the dimension named above; an argument that names none is the same for every part. Nothing has to cross between parts.
Inputs may be any that keep to these rules, and one draw needn't show every extreme that they name: `source`: A permutation of the old slots. Each engine's 16 new slots hold exactly 2 rollouts from each of 3 other engines and 10 rollouts from its own old slots; engine e takes from the engines e - d mod 4 for 3 distances d that are the same for every engine, so every engine also gives exactly 2 rollouts to each of 3 others.
All inputs are finite; a program needn't handle non-finite values.
Results may differ from a plain program's by a relative error of at most 0.008.
Values may be sent and summed in bfloat16 or wider, within the bound.
No kernel may reach another device: no remote copies, remote signals or barrier semaphores. Data moves between devices by JAX's collectives and lax.ppermute only.
A program may use at most 192 MiB of HBM per device.

v0:
```python
import jax
import jax.numpy as jnp
from jax import lax
from jax.sharding import PartitionSpec as P

CAP = 2


def body(
    mr_qkv,
    li_qkv,
    conv_tails,
    modal_states,
    source,
    remaining,
    mr_filter,
    li_decay,
    li_residue,
    mr_panels,
    li_panels,
    panel_slot,
):
    engines = lax.axis_size("engine")
    me = lax.axis_index("engine")
    rows = conv_tails.shape[0]
    tail_len = conv_tails.shape[1]
    width = conv_tails.shape[2]
    panel_cols = mr_panels.shape[2]
    panel_count = panel_slot.shape[0]
    owners = source.reshape(engines, rows)
    engine_ids = jnp.arange(engines, dtype=jnp.int32)
    from_me = (owners // rows == me) & (engine_ids[:, None] != me)
    order_rank = jnp.cumsum(from_me.astype(jnp.int32), axis=1) - 1
    place_ids = jnp.arange(CAP, dtype=jnp.int32)
    picks = from_me[:, :, None] & (order_rank[:, :, None] == place_ids[None, None, :])
    send_index = jnp.sum(picks.astype(jnp.int32) * (owners % rows)[:, :, None], axis=1)
    send_tails = conv_tails[send_index.reshape(-1)].reshape(engines, CAP, tail_len, width)
    send_states = modal_states[send_index.reshape(-1)].reshape(
        engines, CAP, modal_states.shape[1], width
    )
    got_tails = lax.all_to_all(send_tails, "engine", split_axis=0, concat_axis=0, tiled=True)
    got_states = lax.all_to_all(send_states, "engine", split_axis=0, concat_axis=0, tiled=True)
    mine = lax.dynamic_slice_in_dim(source, me * rows, rows)
    src_engine = mine // rows
    src_local = mine % rows
    row_ids = jnp.arange(rows, dtype=jnp.int32)
    earlier = (src_engine[:, None] == src_engine[None, :]) & (row_ids[None, :] < row_ids[:, None])
    arrive_rank = jnp.sum(earlier.astype(jnp.int32), axis=1)
    arrive_index = jnp.clip(src_engine * CAP + arrive_rank, 0, engines * CAP - 1)
    stays = src_engine == me
    tails = jnp.where(
        stays[:, None, None],
        conv_tails[src_local],
        got_tails.reshape(engines * CAP, tail_len, width)[arrive_index],
    )
    states = jnp.where(
        stays[:, None, None],
        modal_states[src_local],
        got_states.reshape(engines * CAP, got_states.shape[2], width)[arrive_index],
    )
    filt = mr_filter.astype(jnp.float32)
    part_first = jnp.einsum("rtc,tc->rc", tails, mr_filter[1:], preferred_element_type=jnp.float32)
    part_second = jnp.einsum(
        "rtc,tc->rc", tails[:, : tail_len - 1], mr_filter[2:], preferred_element_type=jnp.float32
    )
    zmr_first = (mr_qkv[0, 1].astype(jnp.float32) * mr_qkv[0, 2].astype(jnp.float32)).astype(
        jnp.bfloat16
    )
    zmr_second = (mr_qkv[1, 1].astype(jnp.float32) * mr_qkv[1, 2].astype(jnp.float32)).astype(
        jnp.bfloat16
    )
    new_tails = jnp.concatenate(
        [zmr_second[:, None, :], zmr_first[:, None, :], tails[:, : tail_len - 2]], axis=1
    )
    zmr0 = zmr_first.astype(jnp.float32)
    zmr1 = zmr_second.astype(jnp.float32)
    conv0 = filt[0] * zmr0 + part_first
    conv1 = filt[0] * zmr1 + filt[1] * zmr0 + part_second
    ymr0 = (mr_qkv[0, 0].astype(jnp.float32) * conv0).astype(jnp.bfloat16)
    ymr1 = (mr_qkv[1, 0].astype(jnp.float32) * conv1).astype(jnp.bfloat16)
    zli0 = (
        (li_qkv[0, 1].astype(jnp.float32) * li_qkv[0, 2].astype(jnp.float32))
        .astype(jnp.bfloat16)
        .astype(jnp.float32)
    )
    zli1 = (
        (li_qkv[1, 1].astype(jnp.float32) * li_qkv[1, 2].astype(jnp.float32))
        .astype(jnp.bfloat16)
        .astype(jnp.float32)
    )
    states1 = li_decay[None] * states + zli0[:, None, :]
    yli0 = (li_qkv[0, 0].astype(jnp.float32) * jnp.sum(li_residue[None] * states1, axis=1)).astype(
        jnp.bfloat16
    )
    states2 = li_decay[None] * states1 + zli1[:, None, :]
    yli1 = (li_qkv[1, 0].astype(jnp.float32) * jnp.sum(li_residue[None] * states2, axis=1)).astype(
        jnp.bfloat16
    )
    mr_rows = jnp.stack([ymr0, ymr1])
    li_rows = jnp.stack([yli0, yli1])
    mr_piece = lax.all_gather(mr_panels, "engine", axis=0, tiled=True)
    li_piece = lax.all_gather(li_panels, "engine", axis=0, tiled=True)
    upper = jnp.einsum("srd,gdc->srgc", mr_rows, mr_piece, preferred_element_type=jnp.float32)
    lower = jnp.einsum("srd,gdc->srgc", li_rows, li_piece, preferred_element_type=jnp.float32)
    sectioned = upper + lower
    partial_value = jnp.take(sectioned, panel_slot, axis=2).reshape(
        2, rows, panel_count * panel_cols
    )
    summed = lax.psum_scatter(partial_value, "chan", scatter_dimension=2, tiled=True)
    steps_ids = jnp.arange(2, dtype=jnp.int32)
    active = (remaining[None, :] > steps_ids[:, None]).astype(jnp.float32)
    mixed = (summed * active[:, :, None]).astype(jnp.bfloat16)
    return (mixed, new_tails, states2)


def solution(mesh):
    return jax.shard_map(
        body,
        mesh=mesh,
        in_specs=(
            P(None, None, ("group", "engine"), "chan"),
            P(None, None, ("group", "engine"), "chan"),
            P(("group", "engine"), None, "chan"),
            P(("group", "engine"), None, "chan"),
            P("group"),
            P(("group", "engine")),
            P(None, "chan"),
            P(None, "chan"),
            P(None, "chan"),
            P("engine", "chan", None),
            P("engine", "chan", None),
            P(),
        ),
        out_specs=(
            P(None, ("group", "engine"), "chan"),
            P(("group", "engine"), None, "chan"),
            P(("group", "engine"), None, "chan"),
        ),
        check_vma=False,
    )
```

profile of v0, /device:TPU:0, one launch (start us, length us, event | category | flops | bytes accessed | tf_op | source)
XLA Modules:
  0.0 315.2 jit_solution(9834262589492569166)
XLA Ops:
  11.0 4.2 %all-to-all-start.1 = ((f32[4,2,16,2048]{3,2,1,0:T(8,128)}), f32[4,2,16,2048]{3,2,1,0:T(8,128)S(1)}, u32[]{:S(2)}, u32[]{:S(2)}) async-start(f32[4,2,16,2048]{3,2,1,0:T(8,128)} %bitcast.94), calls=%async_computation.1 | async-start | bytes 2097152 | tf_op jit(solution)/shard_map/all_to_all | solution.py:42
  16.1 13.2 %gather_fusion.1 = bf16[8,127,2048]{2,0,1:T(8,128)(2,1)} fusion(bf16[16,127,2048]{2,0,1:T(8,128)(2,1)} %param.14, s32[1024]{0:T(1024)S(1)} %pad_clamp_fusion.2), kind=kCustom, calls=%fused_computation.1 | custom fusion | bytes 8323104 | tf_op jit(solution)/shard_map/gather | solution.py:37
  29.3 9.3 %reshape.365 = bf16[4,2,127,2048]{3,1,0,2:T(2,128)(2,1)} reshape(bf16[8,127,2048]{2,0,1:T(8,128)(2,1)} %gather_fusion.1) | data formatting | bytes 8323072 | tf_op jit(solution)/shard_map/reshape | solution.py:37
  38.6 7.0 %copy.23 = bf16[4,2,127,2048]{3,1,2,0:T(2,128)(2,1)} copy(bf16[4,2,127,2048]{3,1,0,2:T(2,128)(2,1)} %reshape.365) | data formatting | bytes 8323072 | tf_op jit(solution)/shard_map/reshape | solution.py:37
  46.3 5.1 %all-to-all-start = ((bf16[4,2,127,2048]{3,1,2,0:T(2,128)(2,1)}), bf16[4,2,127,2048]{3,1,2,0:T(2,128)(2,1)}, u32[]{:S(2)}, u32[]{:S(2)}) async-start(bf16[4,2,127,2048]{3,1,2,0:T(2,128)(2,1)} %copy.23), calls=%async_computation | async-start | bytes 8323072 | tf_op jit(solution)/shard_map/all_to_all | solution.py:41
  51.4 18.6 %gather_fusion = bf16[16,127,2048]{2,0,1:T(8,128)(2,1)} fusion(bf16[16,127,2048]{2,0,1:T(8,128)(2,1)} %param.14, s32[1024]{0:T(1024)S(1)} %pad_clamp_fusion.3), kind=kCustom, calls=%fused_computation | custom fusion | bytes 16646208 | tf_op jit(solution)/shard_map/gather | solution.py:53
  70.0 2.0 gather_fusion.3
  75.0 2.2 bitcast_convert_fusion.1
  77.2 2.2 bitcast_convert_fusion
  79.4 2.2 gather_fusion.5
  81.6 4.0 %multiply_reduce_fusion.3 = (f32[16,2048]{1,0:T(8,128)S(1)}, f32[16,2048]{1,0:T(8,128)S(1)}, f32[16,16,2048]{2,1,0:T(8,128)}) fusion(f32[16,2048]{1,0:T(8,128)S(1)} %copy-done.7, f32[16,2048]{1,0:T(8,128)S(1)} %get-tuple-element.22, f32[16,16,2048]{2,1,0:T(8,128)S(1)} %copy-done.3, f32[16,16,2048]{2,1,0:T(8,128)} %gather_fusion.5, ...), kind=kLoop, calls=%fused_computation.18 | loop fusion | flops 4653056 | bytes 7077904 | tf_op jit(solution)/shard_map/reduce_sum | solution.py:92
  86.5 58.1 %all-to-all-done = bf16[4,2,127,2048]{3,1,2,0:T(2,128)(2,1)} async-done(((bf16[4,2,127,2048]{3,1,2,0:T(2,128)(2,1)}), bf16[4,2,127,2048]{3,1,2,0:T(2,128)(2,1)}, u32[]{:S(2)}, u32[]{:S(2)}) %all-to-all-start) | async-done | bytes 4161568 | tf_op jit(solution)/shard_map/all_to_all | solution.py:41
  144.6 6.0 %copy.24 = bf16[4,2,127,2048]{3,2,1,0:T(8,128)(2,1)} copy(bf16[4,2,127,2048]{3,1,2,0:T(2,128)(2,1)} %all-to-all-done) | data formatting | bytes 8323072 | tf_op jit(solution)/shard_map/all_to_all | solution.py:41
  150.6 7.1 %gather_fusion.2 = bf16[16,127,2048]{2,1,0:T(8,128)(2,1)} fusion(bf16[8,127,2048]{2,1,0:T(8,128)(2,1)} %bitcast.92, s32[1024]{0:T(1024)} %pad_clamp_fusion.1), kind=kCustom, calls=%fused_computation.2 | custom fusion | bytes 16646208 | tf_op jit(solution)/shard_map/gather | solution.py:54
  157.8 11.0 %multiply_reduce_fusion = (f32[2048,16]{0,1:T(8,128)S(1)}, bf16[16,127,2048]{2,0,1:T(8,128)(2,1)S(1)}) fusion(f32[2048,127]{0,1:T(8,128)S(1)} %copy-done.5, bf16[16,127,2048]{2,0,1:T(8,128)(2,1)} %gather_fusion, bf16[16,127,2048]{2,1,0:T(8,128)(2,1)} %gather_fusion.2, pred[16]{0:T(512)(128)(4,1)S(1)} %copy-done.9), kind=kLoop, calls=%fused_computation.11 | loop fusion | flops 16613376 | bytes 26140688 | tf_op jit(solution)/shard_map/rtc,tc->rc/dot_general | solution.py:62
  168.8 3.3 %copy-done.2 = bf16[16,127,2048]{2,0,1:T(8,128)(2,1)} copy-done((bf16[16,127,2048]{2,0,1:T(8,128)(2,1)}, bf16[16,127,2048]{2,0,1:T(8,128)(2,1)S(1)}, u32[]{:S(2)}) %copy-start.2) | copy-done | bytes 8323096
  172.1 2.4 multiply_reduce_fusion.1
  174.7 11.4 %fusion = f32[2,16,8,512]{3,1,2,0:T(8,128)S(1)} fusion(bf16[8,2048,512]{2,1,0:T(8,128)(2,1)} %all-gather.5.cloned.1.call-done, bf16[1,16,2048]{2,1,0:T(8,128)(2,1)S(1)} %get-tuple-element.20, bf16[1,16,2048]{2,1,0:T(8,128)(2,1)S(1)} %get-tuple-element.19), kind=kOutput, calls=%fused_computation.7 | convolution fusion | flops 537133056 | bytes 17432576 | tf_op jit(solution)/shard_map/srd,gdc->srgc/dot_general | solution.py:104
  186.1 88.8 %all-gather.3.cloned.1.call-done = bf16[8,2048,512]{2,1,0:T(8,128)(2,1)} async-done(((bf16[2,2048,512]{2,1,0:T(8,128)(2,1)}), bf16[8,2048,512]{2,1,0:T(8,128)(2,1)}) %all-gather.3.cloned.1.call-update) | async-done | bytes 16777232 | tf_op jit(solution)/shard_map/all_gather | solution.py:101
  274.9 8.7 %fusion.4 = f32[2,16,8,512]{3,1,2,0:T(8,128)S(1)} fusion(f32[2,16,8,512]{3,1,2,0:T(8,128)S(1)} %fusion, bf16[8,2048,512]{2,1,0:T(8,128)(2,1)} %all-gather.3.cloned.1.call-done, bf16[1,16,2048]{2,1,0:T(8,128)(2,1)S(1)} %get-tuple-element.16, bf16[1,16,2048]{2,1,0:T(8,128)(2,1)S(1)} %get-tuple-element.15), kind=kOutput, calls=%fused_computation.20 | convolution fusion | flops 537264128 | bytes 17956864 | tf_op jit(solution)/shard_map/srd,gdc->srgc/dot_general | solution.py:103
  285.3 8.1 %slice.90 = bf16[16,125,2048]{2,0,1:T(8,128)(2,1)} slice(bf16[16,127,2048]{2,0,1:T(8,128)(2,1)} %copy-done.2), slice={[0:16], [0:125], [0:2048]} | slice | bytes 16384000 | tf_op jit(solution)/shard_map/slice | solution.py:73
  293.4 7.2 %pad_maximum_fusion = bf16[16,127,2048]{2,0,1:T(8,128)(2,1)} fusion(bf16[16,125,2048]{2,0,1:T(8,128)(2,1)} %slice.90, bf16[16,1,2048]{2,0,1:T(8,128)(2,1)S(1)} %get-tuple-element.18, bf16[16,1,2048]{2,0,1:T(8,128)(2,1)S(1)} %get-tuple-element.17), kind=kLoop, calls=%fused_computation.13 | loop fusion | flops 8323072 | bytes 16646144 | tf_op jit(solution)/shard_map/concatenate | solution.py:72
  300.6 6.4 %reduce-scatter.2.cloned.1.call-done = f32[2,16,1024]{2,1,0:T(8,128)} async-done(((f32[2,16,4096]{2,1,0:T(8,128)}), f32[2,16,1024]{2,1,0:T(8,128)}) %reduce-scatter.2.cloned.1.call-update) | async-done | bytes 131088 | tf_op jit(solution)/shard_map/reduce_scatter | solution.py:109
  307.1 1.6 multiply_convert_fusion
  (64 shorter events, 11.1 us)
Async XLA Ops:
  7.2 2.2 copy-start
  7.2 1.5 copy-start.10
  7.2 167.5 %all-gather.5.cloned.1.call-start = ((), (), s32[]{:S(2)}) async-start(), calls=%async_computation.4 | async-start | bytes 20971520 | tf_op jit(solution)/shard_map/all_gather | solution.py:102
  7.9 266.9 %all-gather.3.cloned.1.call-start = ((), (), s32[]{:S(2)}) async-start(), calls=%async_computation.3 | async-start | bytes 20971520 | tf_op jit(solution)/shard_map/all_gather | solution.py:101
  11.0 35.3 %all-to-all-start.1 = ((f32[4,2,16,2048]{3,2,1,0:T(8,128)}), f32[4,2,16,2048]{3,2,1,0:T(8,128)S(1)}, u32[]{:S(2)}, u32[]{:S(2)}) async-start(f32[4,2,16,2048]{3,2,1,0:T(8,128)} %bitcast.94), calls=%async_computation.1 | async-start | bytes 2097152 | tf_op jit(solution)/shard_map/all_to_all | solution.py:42
  29.3 16.9 %copy-start.11 = (s32[8]{0:T(128)S(1)}, s32[8]{0:T(128)}, u32[]{:S(2)}) copy-start(s32[8]{0:T(128)} %param.23) | copy-start | bytes 100
  46.3 98.3 %all-to-all-start = ((bf16[4,2,127,2048]{3,1,2,0:T(2,128)(2,1)}), bf16[4,2,127,2048]{3,1,2,0:T(2,128)(2,1)}, u32[]{:S(2)}, u32[]{:S(2)}) async-start(bf16[4,2,127,2048]{3,1,2,0:T(2,128)(2,1)} %copy.23), calls=%async_computation | async-start | bytes 8323072 | tf_op jit(solution)/shard_map/all_to_all | solution.py:41
  51.3 255.7 %reduce-scatter.2.cloned.1.call-start = ((), (), s32[]{:S(2)}) async-start(), calls=%async_computation.5 | async-start | bytes 655360 | tf_op jit(solution)/shard_map/reduce_scatter | solution.py:109
  70.0 11.6 %copy-start.7 = (f32[16,2048]{1,0:T(8,128)S(1)}, f32[16,2048]{1,0:T(8,128)}, u32[]{:S(2)}) copy-start(f32[16,2048]{1,0:T(8,128)} %param.20) | copy-start | bytes 393220
  72.0 9.6 %copy-start.3 = (f32[16,16,2048]{2,1,0:T(8,128)S(1)}, f32[16,16,2048]{2,1,0:T(8,128)}, u32[]{:S(2)}) copy-start(f32[16,16,2048]{2,1,0:T(8,128)} %gather_fusion.3) | copy-start | bytes 6291460
  150.6 7.2 %copy-start.5 = (f32[2048,127]{0,1:T(8,128)S(1)}, f32[2048,127]{0,1:T(8,128)}, u32[]{:S(2)}) copy-start(f32[2048,127]{0,1:T(8,128)} %bitcast_convert_fusion.1) | copy-start | bytes 3121156
  150.6 7.2 %copy-start.9 = (pred[16]{0:T(512)(128)(4,1)S(1)}, pred[16]{0:T(512)(128)(4,1)}, u32[]{:S(2)}) copy-start(pred[16]{0:T(512)(128)(4,1)} %get-tuple-element.8) | copy-start | bytes 52
  157.8 14.4 %copy-start.4 = (f32[2048,126]{0,1:T(8,128)S(1)}, f32[2048,126]{0,1:T(8,128)}, u32[]{:S(2)}) copy-start(f32[2048,126]{0,1:T(8,128)} %bitcast_convert_fusion) | copy-start | bytes 3096580
  168.8 3.4 %copy-start.2 = (bf16[16,127,2048]{2,0,1:T(8,128)(2,1)}, bf16[16,127,2048]{2,0,1:T(8,128)(2,1)S(1)}, u32[]{:S(2)}) copy-start(bf16[16,127,2048]{2,0,1:T(8,128)(2,1)S(1)} %get-tuple-element.6) | copy-start | bytes 24969220
  168.8 5.8 %copy-start.6 = (bf16[2,3,16,2048]{3,2,1,0:T(8,128)(2,1)S(1)}, bf16[2,3,16,2048]{3,2,1,0:T(8,128)(2,1)}, u32[]{:S(2)}) copy-start(bf16[2,3,16,2048]{3,2,1,0:T(8,128)(2,1)} %param.12) | copy-start | bytes 1179652
  274.9 9.5 %copy-start.8 = (pred[1,4,8,128]{3,1,2,0:T(4,128)(4,1)S(1)}, pred[1,4,8,128]{3,1,2,0:T(4,128)(4,1)}, u32[]{:S(2)}) copy-start(pred[1,4,8,128]{3,1,2,0:T(4,128)(4,1)} %copy.46) | copy-start | bytes 12292
  274.9 10.4 %copy-start.12 = (s32[16]{0:T(128)S(1)}, s32[16]{0:T(128)}, u32[]{:S(2)}) copy-start(s32[16]{0:T(128)} %param.17) | copy-start | bytes 196
  293.4 15.3 %copy-start.1 = (f32[16,16,2048]{2,1,0:T(8,128)S(1)}, f32[16,16,2048]{2,1,0:T(8,128)}, u32[]{:S(2)}) copy-start(f32[16,16,2048]{2,1,0:T(8,128)} %param.15) | copy-start | bytes 6291460
Sparse Core Ops, SparseCore 0:
  9.6 156.7 all-gather.4
  167.9 106.8 all-gather.2
  285.4 21.6 reduce-scatter.1
where the time goes:
time: 316 us; the launch traced here: 315 us
  waiting for transfers between devices  155 us (49%)
  local copies, waits for them, and re-layouts  81 us (26%)
  other arithmetic  36 us (11%)
  matrix products  20.1 us (6%)
  between operations  13.9 us (4%)
  starting transfers between devices  9.4 us (3%)
    all_gather x1, waiting for transfers between devices, body(): mr_piece = lax.all_gather(mr_panels, 'engine', axis=0, tiled=True)  88.8 us
    all_to_all x1, waiting for transfers between devices, body(): lax.all_to_all(send_tails, 'engine', split_axis=0, concat_axis=0, tiled=T...  58.1 us
    gather x1, local copies, waits for them, and re-layouts, body(): conv_tails[src_local]  18.6 us
    reshape x2, local copies, waits for them, and re-layouts, body(): conv_tails[send_index.reshape(-1)].reshape(engines, CAP, tail_len, width)  16.3 us
    gather x1, local copies, waits for them, and re-layouts, body(): conv_tails[send_index.reshape(-1)].reshape(engines, CAP, tail_len, width)  13.2 us
    dot_general x1, matrix products, body(): jnp.einsum('srd,gdc->srgc', li_rows, li_piece, preferred_element_type=jnp...  11.4 us
    dot_general x1, other arithmetic, body(): jnp.einsum('rtc,tc->rc', tails, mr_filter[1:], preferred_element_type=jnp...  11 us
    dot_general x1, matrix products, body(): jnp.einsum('srd,gdc->srgc', mr_rows, mr_piece, preferred_element_type=jnp...  8.7 us
  transfers between devices with their start and end apart: 5, of which 3 were waited for; matrix products, arithmetic and copies ran while one was open for 39% of the time, Pallas kernels for 0%

commit v1 on v0

--- a/solution.py
+++ b/solution.py
@@ -4,6 +4,18 @@
 from jax.sharding import PartitionSpec as P
 
 CAP = 2
+
+
+def gather_by_bits(array, axis, dim):
+    ways, here = (lax.axis_size(axis), lax.axis_index(axis))
+    grown, reach = (array, 1)
+    while reach < ways:
+        theirs = lax.ppermute(grown, axis, [(d, d ^ reach) for d in range(ways)])
+        mine_first = jnp.concatenate([grown, theirs], axis=dim)
+        theirs_first = jnp.concatenate([theirs, grown], axis=dim)
+        grown = jnp.where(here & reach == 0, mine_first, theirs_first)
+        reach = 2 * reach
+    return grown
 
 
 def body(
@@ -98,7 +110,7 @@
     )
     mr_rows = jnp.stack([ymr0, ymr1])
     li_rows = jnp.stack([yli0, yli1])
-    mr_piece = lax.all_gather(mr_panels, "engine", axis=0, tiled=True)
+    mr_piece = gather_by_bits(mr_panels, "engine", 0)
     li_piece = lax.all_gather(li_panels, "engine", axis=0, tiled=True)
     upper = jnp.einsum("srd,gdc->srgc", mr_rows, mr_piece, preferred_element_type=jnp.float32)
     lower = jnp.einsum("srd,gdc->srgc", li_rows, li_piece, preferred_element_type=jnp.float32)

time: 316 us -> 444 us (1.41)
  waiting for transfers between devices: 155 us -> 267 us
  other arithmetic: 36 us -> 47.5 us
    all_to_all x1, waiting for transfers between devices: 0.01 us -> 241 us  [body(): lax.all_to_all(send_states, 'engine', split_axis=0, concat_axis=0, tiled=...]
    all_gather x1 -> x0, waiting for transfers between devices: 88.8 us -> none  [body(): mr_piece = lax.all_gather(mr_panels, 'engine', axis=0, tiled=True)]
    all_to_all x1, waiting for transfers between devices: 58.1 us -> 12.7 us  [body(): lax.all_to_all(send_tails, 'engine', split_axis=0, concat_axis=0, tiled=T...]
    select_n x0 -> x1, other arithmetic: none -> 11.8 us  [gather_by_bits(): grown = jnp.where(here & reach == 0, mine_first, theirs_first)]
    ppermute x0 -> x2, waiting for transfers between devices: none -> 5.78 us  [gather_by_bits(): theirs = lax.ppermute(grown, axis, [(d, d ^ reach) for d in range(ways)])]
  transfers between devices with their start and end apart: 5 -> 6, of which waited for: 3 -> 4; matrix products, arithmetic and copies ran while one was open for 39% -> 29% of each run, Pallas kernels for 0% -> 0%
where the time goes in v1:
time: 444 us; the launch traced here: 443 us
  waiting for transfers between devices  267 us (60%)
  local copies, waits for them, and re-layouts  80.4 us (18%)
  other arithmetic  47.5 us (11%)
  matrix products  21.1 us (5%)
  between operations  14.2 us (3%)
  starting transfers between devices  12.5 us (3%)
    all_to_all x1, waiting for transfers between devices, body(): lax.all_to_all(send_states, 'engine', split_axis=0, concat_axis=0, tiled=...  241 us
    gather x1, local copies, waits for them, and re-layouts, body(): conv_tails[src_local]  18.4 us
    reshape x2, local copies, waits for them, and re-layouts, body(): conv_tails[send_index.reshape(-1)].reshape(engines, CAP, tail_len, width)  16.3 us
    all_to_all x1, waiting for transfers between devices, body(): lax.all_to_all(send_tails, 'engine', split_axis=0, concat_axis=0, tiled=T...  12.7 us
    dot_general x1, matrix products, body(): jnp.einsum('srd,gdc->srgc', mr_rows, mr_piece, preferred_element_type=jnp...  12.4 us
    gather x1, local copies, waits for them, and re-layouts, body(): conv_tails[send_index.reshape(-1)].reshape(engines, CAP, tail_len, width)  12.1 us
    select_n x1, other arithmetic, gather_by_bits(): grown = jnp.where(here & reach == 0, mine_first, theirs_first)  11.8 us
    dot_general x1, other arithmetic, body(): jnp.einsum('rtc,tc->rc', tails, mr_filter[1:], preferred_element_type=jnp...  10.8 us
  transfers between devices with their start and end apart: 6, of which 4 were waited for; matrix products, arithmetic and copies ran while one was open for 29% of the time, Pallas kernels for 0%

profile of v1, /device:TPU:0, one launch (start us, length us, event | category | flops | bytes accessed | tf_op | source)
XLA Modules:
  0.0 442.7 jit_solution(2299293335546663657)
XLA Ops:
  9.8 5.8 %collective-permute-done = bf16[2,2048,512]{2,1,0:T(8,128)(2,1)} collective-permute-done((bf16[2,2048,512]{2,1,0:T(8,128)(2,1)}, bf16[2,2048,512]{2,1,0:T(8,128)(2,1)}, u32[]{:S(2)}, u32[]{:S(2)}) %collective-permute-start) | collective-permute-done | bytes 4194336 | tf_op jit(solution)/shard_map/ppermute | solution.py:13
  15.6 11.8 %maximum_select_fusion.1 = bf16[4,2048,512]{2,1,0:T(8,128)(2,1)} fusion(bf16[2,2048,512]{2,1,0:T(8,128)(2,1)} %collective-permute-done, bf16[2,2048,512]{2,1,0:T(8,128)(2,1)} %param.21, pred[]{:T(512)S(6)} %eq.67), kind=kLoop, calls=%fused_computation.15 | loop fusion | flops 12582912 | bytes 16777216 | tf_op jit(solution)/shard_map/jit(_where)/select_n | solution.py:16
  27.3 3.3 collective-permute-start.1
  32.3 3.5 all-to-all-start.1
  36.6 12.1 %gather_fusion.1 = bf16[8,127,2048]{2,0,1:T(8,128)(2,1)} fusion(bf16[16,127,2048]{2,0,1:T(8,128)(2,1)} %param.14, s32[1024]{0:T(1024)S(1)} %pad_clamp_fusion.2), kind=kCustom, calls=%fused_computation.1 | custom fusion | bytes 8323104 | tf_op jit(solution)/shard_map/gather | solution.py:49
  48.7 9.2 %reshape.365 = bf16[4,2,127,2048]{3,1,0,2:T(2,128)(2,1)} reshape(bf16[8,127,2048]{2,0,1:T(8,128)(2,1)} %gather_fusion.1) | data formatting | bytes 8323072 | tf_op jit(solution)/shard_map/reshape | solution.py:49
  58.0 7.0 %copy.23 = bf16[4,2,127,2048]{3,1,2,0:T(2,128)(2,1)} copy(bf16[4,2,127,2048]{3,1,0,2:T(2,128)(2,1)} %reshape.365) | data formatting | bytes 8323072 | tf_op jit(solution)/shard_map/reshape | solution.py:49
  65.7 241.4 %all-to-all-done.1 = f32[4,2,16,2048]{3,2,1,0:T(8,128)S(1)} async-done(((f32[4,2,16,2048]{3,2,1,0:T(8,128)}), f32[4,2,16,2048]{3,2,1,0:T(8,128)S(1)}, u32[]{:S(2)}, u32[]{:S(2)}) %all-to-all-start.1) | async-done | bytes 1048608 | tf_op jit(solution)/shard_map/all_to_all | solution.py:54
  307.1 4.9 %all-to-all-start = ((bf16[4,2,127,2048]{3,1,2,0:T(2,128)(2,1)}), bf16[4,2,127,2048]{3,1,2,0:T(2,128)(2,1)}, u32[]{:S(2)}, u32[]{:S(2)}) async-start(bf16[4,2,127,2048]{3,1,2,0:T(2,128)(2,1)} %copy.23), calls=%async_computation | async-start | bytes 8323072 | tf_op jit(solution)/shard_map/all_to_all | solution.py:53
  312.2 18.4 %gather_fusion = bf16[16,127,2048]{2,0,1:T(8,128)(2,1)} fusion(bf16[16,127,2048]{2,0,1:T(8,128)(2,1)} %param.14, s32[1024]{0:T(1024)S(1)} %pad_clamp_fusion.3), kind=kCustom, calls=%fused_computation | custom fusion | bytes 16646208 | tf_op jit(solution)/shard_map/gather | solution.py:65
  335.7 2.2 bitcast_convert_fusion.1
  337.9 2.2 bitcast_convert_fusion
  342.2 4.0 multiply_reduce_fusion.3
  347.1 12.7 %all-to-all-done = bf16[4,2,127,2048]{3,1,2,0:T(2,128)(2,1)} async-done(((bf16[4,2,127,2048]{3,1,2,0:T(2,128)(2,1)}), bf16[4,2,127,2048]{3,1,2,0:T(2,128)(2,1)}, u32[]{:S(2)}, u32[]{:S(2)}) %all-to-all-start) | async-done | bytes 4161568 | tf_op jit(solution)/shard_map/all_to_all | solution.py:53
  359.8 6.0 %copy.24 = bf16[4,2,127,2048]{3,2,1,0:T(8,128)(2,1)} copy(bf16[4,2,127,2048]{3,1,2,0:T(2,128)(2,1)} %all-to-all-done) | data formatting | bytes 8323072 | tf_op jit(solution)/shard_map/all_to_all | solution.py:53
  365.8 7.1 %gather_fusion.2 = bf16[16,127,2048]{2,1,0:T(8,128)(2,1)} fusion(bf16[8,127,2048]{2,1,0:T(8,128)(2,1)} %bitcast.92, s32[1024]{0:T(1024)} %pad_clamp_fusion.1), kind=kCustom, calls=%fused_computation.2 | custom fusion | bytes 16646208 | tf_op jit(solution)/shard_map/gather | solution.py:66
  373.0 10.8 %multiply_reduce_fusion = (f32[2048,16]{0,1:T(8,128)S(1)}, bf16[16,127,2048]{2,0,1:T(8,128)(2,1)S(1)}) fusion(f32[2048,127]{0,1:T(8,128)S(1)} %copy-done.5, bf16[16,127,2048]{2,0,1:T(8,128)(2,1)} %gather_fusion, bf16[16,127,2048]{2,1,0:T(8,128)(2,1)} %gather_fusion.2, pred[16]{0:T(512)(128)(4,1)S(1)} %copy-done.9), kind=kLoop, calls=%fused_computation.13 | loop fusion | flops 16613376 | bytes 26140688 | tf_op jit(solution)/shard_map/rtc,tc->rc/dot_general | solution.py:74
  383.8 3.3 copy-done.2
  387.2 2.4 multiply_reduce_fusion.1
  389.7 8.7 %fusion.1 = f32[2,16,8,512]{3,1,2,0:T(8,128)S(1)} fusion(bf16[8,2048,512]{2,1,0:T(8,128)(2,1)} %all-gather.2.cloned.1.call-done, bf16[1,16,2048]{2,1,0:T(8,128)(2,1)S(1)} %get-tuple-element.20, bf16[1,16,2048]{2,1,0:T(8,128)(2,1)S(1)} %get-tuple-element.19), kind=kOutput, calls=%fused_computation.9 | convolution fusion | flops 537133056 | bytes 17432576 | tf_op jit(solution)/shard_map/srd,gdc->srgc/dot_general | solution.py:116
  398.4 12.4 %fusion.6 = f32[2,16,8,512]{3,1,2,0:T(8,128)S(1)} fusion(f32[2,16,8,512]{3,1,2,0:T(8,128)S(1)} %fusion.1, bf16[4,2048,512]{2,1,0:T(8,128)(2,1)} %collective-permute-done.1, bf16[4,2048,512]{2,1,0:T(8,128)(2,1)} %maximum_select_fusion.1, pred[]{:T(512)S(6)} %eq.66, bf16[1,16,2048]{2,1,0:T(8,128)(2,1)S(1)} %get-tuple-element.16, ...), kind=kOutput, calls=%fused_computation.23 | convolution fusion | flops 612761600 | bytes 17956864 | tf_op jit(solution)/shard_map/srd,gdc->srgc/dot_general | solution.py:115
  412.5 8.1 %slice.90 = bf16[16,125,2048]{2,0,1:T(8,128)(2,1)} slice(bf16[16,127,2048]{2,0,1:T(8,128)(2,1)} %copy-done.2), slice={[0:16], [0:125], [0:2048]} | slice | bytes 16384000 | tf_op jit(solution)/shard_map/slice | solution.py:85
  420.6 7.2 %pad_maximum_fusion = bf16[16,127,2048]{2,0,1:T(8,128)(2,1)} fusion(bf16[16,125,2048]{2,0,1:T(8,128)(2,1)} %slice.90, bf16[16,1,2048]{2,0,1:T(8,128)(2,1)S(1)} %get-tuple-element.18, bf16[16,1,2048]{2,0,1:T(8,128)(2,1)S(1)} %get-tuple-element.17), kind=kLoop, calls=%fused_computation.16 | loop fusion | flops 8323072 | bytes 16646144 | tf_op jit(solution)/shard_map/concatenate | solution.py:84
  427.8 6.4 %reduce-scatter.2.cloned.1.call-done = f32[2,16,1024]{2,1,0:T(8,128)} async-done(((f32[2,16,4096]{2,1,0:T(8,128)}), f32[2,16,1024]{2,1,0:T(8,128)}) %reduce-scatter.2.cloned.1.call-update) | async-done | bytes 131088 | tf_op jit(solution)/shard_map/reduce_scatter | solution.py:121
  (67 shorter events, 17.4 us)
Async XLA Ops:
  7.2 23.5 %copy-start = (f32[16,16,2048]{2,1,0:T(8,128)S(1)}, f32[16,16,2048]{2,1,0:T(8,128)}, u32[]{:S(2)}) copy-start(f32[16,16,2048]{2,1,0:T(8,128)} %param.15) | copy-start | bytes 6291460
  7.2 382.5 %all-gather.2.cloned.1.call-start = ((), (), s32[]{:S(2)}) async-start(), calls=%async_computation.3 | async-start | bytes 20971520 | tf_op jit(solution)/shard_map/all_gather | solution.py:114
  7.9 7.6 %collective-permute-start = (bf16[2,2048,512]{2,1,0:T(8,128)(2,1)}, bf16[2,2048,512]{2,1,0:T(8,128)(2,1)}, u32[]{:S(2)}, u32[]{:S(2)}) collective-permute-start(bf16[2,2048,512]{2,1,0:T(8,128)(2,1)} %param.21), channel_id=1, source_target_pairs={{0,4},{4,0},{8,12},{12,8},{1,5},{5,1},{9,13},{13,9},{2,6},{6,2},{1... | collective-permute-start | bytes 12582920 | tf_op jit(solution)/shard_map/ppermute | solution.py:13
  9.8 26.0 %copy-start.10 = (s32[64]{0:T(128)S(1)}, s32[64]{0:T(128)}, u32[]{:S(2)}) copy-start(s32[64]{0:T(128)} %param.16) | copy-start | bytes 772
  27.3 371.0 %collective-permute-start.1 = (bf16[4,2048,512]{2,1,0:T(8,128)(2,1)}, bf16[4,2048,512]{2,1,0:T(8,128)(2,1)}, u32[]{:S(2)}, u32[]{:S(2)}) collective-permute-start(bf16[4,2048,512]{2,1,0:T(8,128)(2,1)} %maximum_select_fusion.1), channel_id=1, source_target_pairs={{0,8},{4,12},{8,0},{12,4},{1,9},{5,13},{9,1},{13,5},{2,10},{6,14},... | collective-permute-start | bytes 25165832 | tf_op jit(solution)/shard_map/ppermute | solution.py:13
  32.3 274.8 %all-to-all-start.1 = ((f32[4,2,16,2048]{3,2,1,0:T(8,128)}), f32[4,2,16,2048]{3,2,1,0:T(8,128)S(1)}, u32[]{:S(2)}, u32[]{:S(2)}) async-start(f32[4,2,16,2048]{3,2,1,0:T(8,128)} %bitcast.94), calls=%async_computation.1 | async-start | bytes 2097152 | tf_op jit(solution)/shard_map/all_to_all | solution.py:54
  48.7 16.9 %copy-start.11 = (s32[8]{0:T(128)S(1)}, s32[8]{0:T(128)}, u32[]{:S(2)}) copy-start(s32[8]{0:T(128)} %param.23) | copy-start | bytes 100
  307.1 52.7 %all-to-all-start = ((bf16[4,2,127,2048]{3,1,2,0:T(2,128)(2,1)}), bf16[4,2,127,2048]{3,1,2,0:T(2,128)(2,1)}, u32[]{:S(2)}, u32[]{:S(2)}) async-start(bf16[4,2,127,2048]{3,1,2,0:T(2,128)(2,1)} %copy.23), calls=%async_computation | async-start | bytes 8323072 | tf_op jit(solution)/shard_map/all_to_all | solution.py:53
  311.9 122.3 %reduce-scatter.2.cloned.1.call-start = ((), (), s32[]{:S(2)}) async-start(), calls=%async_computation.4 | async-start | bytes 655360 | tf_op jit(solution)/shard_map/reduce_scatter | solution.py:121
  330.6 11.5 %copy-start.7 = (f32[16,2048]{1,0:T(8,128)S(1)}, f32[16,2048]{1,0:T(8,128)}, u32[]{:S(2)}) copy-start(f32[16,2048]{1,0:T(8,128)} %param.20) | copy-start | bytes 393220
  332.6 9.5 %copy-start.3 = (f32[16,16,2048]{2,1,0:T(8,128)S(1)}, f32[16,16,2048]{2,1,0:T(8,128)}, u32[]{:S(2)}) copy-start(f32[16,16,2048]{2,1,0:T(8,128)} %gather_fusion.3) | copy-start | bytes 6291460
  365.8 7.1 %copy-start.5 = (f32[2048,127]{0,1:T(8,128)S(1)}, f32[2048,127]{0,1:T(8,128)}, u32[]{:S(2)}) copy-start(f32[2048,127]{0,1:T(8,128)} %bitcast_convert_fusion.1) | copy-start | bytes 3121156
  365.8 7.1 %copy-start.9 = (pred[16]{0:T(512)(128)(4,1)S(1)}, pred[16]{0:T(512)(128)(4,1)}, u32[]{:S(2)}) copy-start(pred[16]{0:T(512)(128)(4,1)} %get-tuple-element.8) | copy-start | bytes 52
  373.0 14.2 %copy-start.4 = (f32[2048,126]{0,1:T(8,128)S(1)}, f32[2048,126]{0,1:T(8,128)}, u32[]{:S(2)}) copy-start(f32[2048,126]{0,1:T(8,128)} %bitcast_convert_fusion) | copy-start | bytes 3096580
  383.8 3.4 copy-start.2
  383.8 5.8 %copy-start.6 = (bf16[2,3,16,2048]{3,2,1,0:T(8,128)(2,1)S(1)}, bf16[2,3,16,2048]{3,2,1,0:T(8,128)(2,1)}, u32[]{:S(2)}) copy-start(bf16[2,3,16,2048]{3,2,1,0:T(8,128)(2,1)} %param.12) | copy-start | bytes 1179652
  398.4 13.2 %copy-start.8 = (pred[1,4,8,128]{3,1,2,0:T(4,128)(4,1)S(1)}, pred[1,4,8,128]{3,1,2,0:T(4,128)(4,1)}, u32[]{:S(2)}) copy-start(pred[1,4,8,128]{3,1,2,0:T(4,128)(4,1)} %copy.46) | copy-start | bytes 12292
  398.4 14.1 %copy-start.12 = (s32[16]{0:T(128)S(1)}, s32[16]{0:T(128)}, u32[]{:S(2)}) copy-start(s32[16]{0:T(128)} %param.17) | copy-start | bytes 196
  420.6 15.2 %copy-start.1 = (f32[16,16,2048]{2,1,0:T(8,128)S(1)}, f32[16,16,2048]{2,1,0:T(8,128)}, u32[]{:S(2)}) copy-start(f32[16,16,2048]{2,1,0:T(8,128)} %param.15) | copy-start | bytes 6291460
Sparse Core Ops, SparseCore 0:
  9.6 192.9 all-gather.1
  412.6 21.6 reduce-scatter.1
